TPU v7x, 256 devices: a whole 4x4x8 slice. The times are simulated.
256 devices in a mesh: dp: 32 (over z, y_hi, core), owner: 8 (over y_lo, x).
Axes of the slice: x: 4, y: 4 (y_hi: 2, y_lo: 2; y = y_hi * 2 + y_lo), z: 8, core: 2. Of those that a mesh axis runs over, the one named last changes fastest.
Arguments:
- inputs: bfloat16 [4096, 8192], P('dp'), may hold values from -12 to 12
- out_grads: bfloat16 [4096, 8192], P('dp', 'owner'), may hold values from -16 to 16
- weights: float32 [256, 512, 512], P(('dp', 'owner')), may hold values from -0.0625 to 0.0625
- left_stats: float32 [256, 512, 512], P(('dp', 'owner')), as said below
- right_stats: float32 [256, 512, 512], P(('dp', 'owner')), as said below
- left_roots: float32 [256, 512, 512], P(('dp', 'owner')), as said below
- right_roots: float32 [256, 512, 512], P(('dp', 'owner')), as said below
- refresh: int32 [256], P(('dp', 'owner')), may hold values from 0 to 1, as said below
Outputs:
- new_left_stats: float32 [256, 512, 512], P(('dp', 'owner'))
- new_right_stats: float32 [256, 512, 512], P(('dp', 'owner'))
- new_left_roots: float32 [256, 512, 512], P(('dp', 'owner'))
- new_right_roots: float32 [256, 512, 512], P(('dp', 'owner'))
- update: float32 [256, 512, 512], P(('dp', 'owner'))
- queries: bfloat16 [4096, 8192], P('dp', 'owner')
Inputs may be any that keep to these rules, and one draw needn't show every extreme that they name: For every k, refresh[2k] + refresh[2k + 1] is at most 1, and refresh[0] + refresh[1] is 1. `left_stats`: every block is symmetric positive definite. `right_stats`: every block is symmetric positive definite. `left_roots`: every block is symmetric positive definite. `right_roots`: every block is symmetric positive definite.
All inputs are finite; a program needn't handle non-finite values.
Results may differ from a plain program's by a relative error of at most 0.015.
Values may be sent and summed in bfloat16 or wider, within the bound.
No kernel may reach another device: no remote copies, remote signals or barrier semaphores. Data moves between devices by JAX's collectives and lax.ppermute only.
A program may use at most 128 MiB of HBM per device.

v0:
```python
import math
import jax
import jax.numpy as jnp
from jax import lax
from jax.sharding import PartitionSpec as P

NEWTON = 2
BETA = 0.95
DAMPING = 0.0001


def matmul(left_mat, right_mat):
    return jnp.dot(left_mat, right_mat, preferred_element_type=jnp.float32)


def inverse_root(statistic):
    identity = jnp.eye(statistic.shape[0], dtype=jnp.float32)
    damped = statistic + DAMPING * identity
    factor_z = 2.5 / jnp.sqrt(jnp.sum(damped * damped))
    current = factor_z * damped
    result = jnp.sqrt(jnp.sqrt(factor_z)) * identity
    for turn in range(NEWTON):
        factor = 1.25 * identity - 0.25 * current
        result = matmul(result, factor)
        square = matmul(factor, factor)
        current = matmul(matmul(square, square), current)
    return result


def both_roots(left_stat, right_stat, left_old, right_old):
    return (inverse_root(left_stat), inverse_root(right_stat))


def stale_roots(left_stat, right_stat, left_old, right_old):
    return (left_old, right_old)


def body(inputs, out_grads, weights, left_stats, right_stats, left_roots, right_roots, refresh):
    tok_local, model_width = inputs.shape
    block_size = weights.shape[1]
    col_count = out_grads.shape[1]
    row_blocks = model_width // block_size
    col_blocks = col_count // block_size
    replicas = lax.axis_size("dp")
    tok_total = tok_local * replicas
    x_blocks = inputs.reshape(tok_local, row_blocks, block_size)
    g_blocks = out_grads.reshape(tok_local, col_blocks, block_size)
    feature_send = jnp.repeat(x_blocks, col_blocks, axis=1)
    grad_send = jnp.tile(g_blocks, (1, row_blocks, 1))
    feature_recv, grad_recv = (
        lax.all_to_all(feature_send, "dp", split_axis=1, concat_axis=1, tiled=True),
        lax.all_to_all(grad_send, "dp", split_axis=1, concat_axis=1, tiled=True),
    )
    group_size = 4

    def add_group(turn_index, running):
        x_group = lax.dynamic_slice_in_dim(feature_recv, turn_index * group_size, group_size, 1)
        g_group = lax.dynamic_slice_in_dim(grad_recv, turn_index * group_size, group_size, 1)
        products = (
            jnp.einsum("tsb,tsc->sbc", x_group, g_group, preferred_element_type=jnp.float32)
            / tok_total
        )
        products = lax.optimization_barrier(products.astype(jnp.bfloat16))
        return running + jnp.sum(products.astype(jnp.float32), 0)

    gradient = lax.fori_loop(
        0, replicas // group_size, add_group, jnp.zeros((block_size, block_size), jnp.float32)
    )
    left_new = BETA * left_stats[0] + (1.0 - BETA) * matmul(gradient, gradient.T)
    right_new = BETA * right_stats[0] + (1.0 - BETA) * matmul(gradient.T, gradient)
    refreshing = refresh[0] > 0
    left_root, right_root = lax.cond(
        refreshing, both_roots, stale_roots, left_new, right_new, left_roots[0], right_roots[0]
    )
    direction = matmul(matmul(left_root, gradient), right_root)
    direction = direction * (block_size / jnp.sqrt(jnp.sum(direction * direction) + 1e-12))
    rate = 0.25 / math.sqrt(model_width)
    updated = (weights[0] - rate * direction).astype(jnp.bfloat16)
    partial_out = jnp.einsum(
        "tsb,bc->tsc", feature_recv, updated, preferred_element_type=jnp.float32
    )
    returned = lax.all_to_all(
        partial_out.astype(jnp.bfloat16), "dp", split_axis=1, concat_axis=1, tiled=True
    ).astype(partial_out.dtype)
    queries = returned.reshape(tok_local, row_blocks, col_blocks, block_size).sum(1)
    queries = queries.reshape(tok_local, col_count).astype(jnp.bfloat16)
    return (
        left_new[None],
        right_new[None],
        left_root[None],
        right_root[None],
        direction[None],
        queries,
    )


def solution(mesh):
    in_specs = (
        P("dp", None),
        P("dp", "owner"),
        P(("dp", "owner"), None, None),
        P(("dp", "owner"), None, None),
        P(("dp", "owner"), None, None),
        P(("dp", "owner"), None, None),
        P(("dp", "owner"), None, None),
        P(("dp", "owner")),
    )
    out_specs = (
        P(("dp", "owner"), None, None),
        P(("dp", "owner"), None, None),
        P(("dp", "owner"), None, None),
        P(("dp", "owner"), None, None),
        P(("dp", "owner"), None, None),
        P("dp", "owner"),
    )
    return jax.shard_map(body, mesh=mesh, in_specs=in_specs, out_specs=out_specs, check_vma=False)
```

profile of v0, /device:TPU:4, one launch (start us, length us, event | category | flops | bytes accessed | tf_op | source)
XLA Modules:
  0.0 379.6 jit_solution(8345739376024094570)
XLA Ops:
  0.6 2.4 copy.53
  3.3 2.5 broadcast_in_dim.26
  5.8 11.7 %all-to-all-start = ((bf16[128,32,512]{2,0,1:T(8,128)(2,1)}), bf16[128,32,512]{2,0,1:T(8,128)(2,1)}, u32[]{:S(2)}, u32[]{:S(2)}) async-start(bf16[128,32,512]{2,0,1:T(8,128)(2,1)} %bitcast.52), calls=%async_computation | async-start | bytes 8388608 | tf_op jit(solution)/shard_map/all_to_all | solution.py:51
  17.6 96.7 %all-to-all-done = bf16[128,32,512]{2,0,1:T(8,128)(2,1)} async-done(((bf16[128,32,512]{2,0,1:T(8,128)(2,1)}), bf16[128,32,512]{2,0,1:T(8,128)(2,1)}, u32[]{:S(2)}, u32[]{:S(2)}) %all-to-all-start) | async-done | bytes 4194336 | tf_op jit(solution)/shard_map/all_to_all | solution.py:51
  114.2 2.4 tile.11
  116.6 4.9 %all-to-all-start.1 = ((bf16[128,32,512]{2,0,1:T(8,128)(2,1)}), bf16[128,32,512]{2,0,1:T(8,128)(2,1)}, u32[]{:S(2)}, u32[]{:S(2)}) async-start(bf16[128,32,512]{2,0,1:T(8,128)(2,1)} %bitcast.51), calls=%async_computation.1 | async-start | bytes 8388608 | tf_op jit(solution)/shard_map/all_to_all | solution.py:52
  122.2 96.0 %all-to-all-done.1 = bf16[128,32,512]{2,0,1:T(8,128)(2,1)} async-done(((bf16[128,32,512]{2,0,1:T(8,128)(2,1)}), bf16[128,32,512]{2,0,1:T(8,128)(2,1)}, u32[]{:S(2)}, u32[]{:S(2)}) %all-to-all-start.1) | async-done | bytes 4194336 | tf_op jit(solution)/shard_map/all_to_all | solution.py:52
  218.2 21.4 %while.14 = (s32[]{:T(128)}, f32[512,512]{1,0:T(8,128)S(1)}, bf16[128,32,512]{2,0,1:T(8,128)(2,1)}, bf16[128,32,512]{2,0,1:T(8,128)(2,1)}, s32[]{:T(128)}, /*index=5*/s32[]{:T(128)}, s32[]{:T(128)}, s32[]{:T(128)}) while((s32[]{:T(128)}, f32[512,512]{1,0:T(8,128)S(1)}, bf16[128,32,512]{2,0,1:T(8,128)(2,1)}, ...), condition=%wide.region_2.0_spmd.clone, body=%wide.region_0.0_spmd.clone.sunk | while | flops 272891904 | bytes 9438349 | solution.py:66
  218.2 2.0 multiply_convert_fusion.2
  220.9 2.0 multiply_convert_fusion.2
  223.6 2.0 multiply_convert_fusion.2
  226.2 2.0 multiply_convert_fusion.2
  228.9 2.0 multiply_convert_fusion.2
  231.6 2.0 multiply_convert_fusion.2
  234.3 2.0 multiply_convert_fusion.2
  236.9 2.0 multiply_convert_fusion.2
  239.6 1.8 fusion.98
  243.0 2.2 conditional.1
  243.0 1.2 copy.42
  246.1 2.7 multiply_reduce_fusion.2
  249.5 6.9 %convert_bitcast_fusion = bf16[128,32,512]{0,2,1:T(8,128)(2,1)} fusion(bf16[128,32,512]{2,0,1:T(8,128)(2,1)} %all-to-all-done, f32[512,512]{1,0:T(8,128)S(1)} %get-tuple-element.156, f32[1,512,512]{2,1,0:T(8,128)} %param.14, f32[]{:T(128)S(6)} %div.14), kind=kOutput, calls=%fused_computation.69 | convolution fusion | flops 2150629376 | bytes 10485764 | tf_op jit(solution)/shard_map/tsb,bc->tsc/dot_general | solution.py:79
  256.4 22.7 %all-to-all-start.2 = ((bf16[128,32,512]{0,2,1:T(8,128)(2,1)}), bf16[128,32,512]{0,2,1:T(8,128)(2,1)}, u32[]{:S(2)}, u32[]{:S(2)}) async-start(bf16[128,32,512]{0,2,1:T(8,128)(2,1)} %convert_bitcast_fusion), calls=%async_computation.2 | async-start | bytes 8388608 | tf_op jit(solution)/shard_map/all_to_all | solution.py:82
  280.2 95.6 %all-to-all-done.2 = bf16[128,32,512]{0,2,1:T(8,128)(2,1)} async-done(((bf16[128,32,512]{0,2,1:T(8,128)(2,1)}), bf16[128,32,512]{0,2,1:T(8,128)(2,1)}, u32[]{:S(2)}, u32[]{:S(2)}) %all-to-all-start.2) | async-done | bytes 4194336 | tf_op jit(solution)/shard_map/all_to_all | solution.py:82
  375.8 2.9 reduce
  (37 shorter events, 11.0 us)
Async XLA Ops:
  0.6 2.4 copy-start.7
  5.8 11.8 %copy-start.10 = (bf16[128,1024]{1,0:T(8,128)(2,1)S(1)}, bf16[128,1024]{1,0:T(8,128)(2,1)}, u32[]{:S(2)}) copy-start(bf16[128,1024]{1,0:T(8,128)(2,1)} %param.13) | copy-start | bytes 786436
  5.8 108.4 %all-to-all-start = ((bf16[128,32,512]{2,0,1:T(8,128)(2,1)}), bf16[128,32,512]{2,0,1:T(8,128)(2,1)}, u32[]{:S(2)}, u32[]{:S(2)}) async-start(bf16[128,32,512]{2,0,1:T(8,128)(2,1)} %bitcast.52), calls=%async_computation | async-start | bytes 8388608 | tf_op jit(solution)/shard_map/all_to_all | solution.py:51
  116.6 101.6 %all-to-all-start.1 = ((bf16[128,32,512]{2,0,1:T(8,128)(2,1)}), bf16[128,32,512]{2,0,1:T(8,128)(2,1)}, u32[]{:S(2)}, u32[]{:S(2)}) async-start(bf16[128,32,512]{2,0,1:T(8,128)(2,1)} %bitcast.51), calls=%async_computation.1 | async-start | bytes 8388608 | tf_op jit(solution)/shard_map/all_to_all | solution.py:52
  239.6 1.9 copy-start.9
  239.6 2.4 copy-start.2
  241.5 1.0 copy-start.3
  242.0 1.0 copy-start.4
  245.2 1.0 copy-start.8
  256.4 119.4 %all-to-all-start.2 = ((bf16[128,32,512]{0,2,1:T(8,128)(2,1)}), bf16[128,32,512]{0,2,1:T(8,128)(2,1)}, u32[]{:S(2)}, u32[]{:S(2)}) async-start(bf16[128,32,512]{0,2,1:T(8,128)(2,1)} %convert_bitcast_fusion), calls=%async_computation.2 | async-start | bytes 8388608 | tf_op jit(solution)/shard_map/all_to_all | solution.py:82
where the time goes:
time: 380 us
  waiting for transfers between devices  288 us (76%)
  starting transfers between devices  39.3 us (10%)
  matrix products  27.6 us (7%)
  local copies, waits for them, and re-layouts  12.6 us (3%)
  other arithmetic  9.34 us (2%)
    all_to_all x1, waiting for transfers between devices, body(): lax.all_to_all(feature_send, 'dp', split_axis=1, concat_axis=1, tiled=True)  96.7 us
    all_to_all x1, waiting for transfers between devices, body(): lax.all_to_all(grad_send, 'dp', split_axis=1, concat_axis=1, tiled=True)  96 us
    all_to_all x1, waiting for transfers between devices, body(): lax.all_to_all(partial_out.astype(jnp.bfloat16), 'dp', split_axis=1, conc...  95.6 us
    all_to_all x1, starting transfers between devices, body(): lax.all_to_all(partial_out.astype(jnp.bfloat16), 'dp', split_axis=1, conc...  22.7 us
    dot_general x8, matrix products, add_group(): jnp.einsum('tsb,tsc->sbc', x_group, g_group, preferred_element_type=jnp.f...  15.6 us
    all_to_all x1, starting transfers between devices, body(): lax.all_to_all(feature_send, 'dp', split_axis=1, concat_axis=1, tiled=True)  11.7 us
  transfers between devices with their start and end apart: 3, of which 3 were waited for; matrix products, arithmetic and copies ran while one was open for 0% of the time, Pallas kernels for 0%

commit v1 on v0

--- a/solution.py
+++ b/solution.py
@@ -1,3 +1,4 @@
+import functools
 import math
 import jax
 import jax.numpy as jnp
@@ -7,6 +8,16 @@
 NEWTON = 2
 BETA = 0.95
 DAMPING = 0.0001
+
+
+def supply_all_records(shard_in, array_axis, at_axis):
+    val2 = jnp.stack(jnp.split(shard_in, jax.lax.axis_size("dp"), array_axis))
+    placed = jax.lax.all_to_all(val2, "dp", 0, 0)
+    m_next = jnp.concatenate(placed, at_axis)
+    return m_next
+
+
+take_the_page = functools.partial(supply_all_records, array_axis=1, at_axis=1)
 
 
 def matmul(left_mat, right_mat):
@@ -49,7 +60,7 @@
     grad_send = jnp.tile(g_blocks, (1, row_blocks, 1))
     feature_recv, grad_recv = (
         lax.all_to_all(feature_send, "dp", split_axis=1, concat_axis=1, tiled=True),
-        lax.all_to_all(grad_send, "dp", split_axis=1, concat_axis=1, tiled=True),
+        take_the_page(grad_send),
     )
     group_size = 4
 

time: 380 us -> 398 us (1.047)
  local copies, waits for them, and re-layouts: 12.6 us -> 33.1 us
    unnamed x16 -> x45, local copies, waits for them, and re-layouts: 5.21 us -> 25.5 us
    all_to_all x1, starting transfers between devices: 11.7 us -> 4.89 us  [body(): lax.all_to_all(feature_send, 'dp', split_axis=1, concat_axis=1, tiled=True)]
    all_to_all x1, starting transfers between devices: 4.89 us -> 11.6 us  [supply_all_records(): placed = jax.lax.all_to_all(val2, 'dp', 0, 0)]
  transfers between devices with their start and end apart: 3 -> 3, of which waited for: 3 -> 3; matrix products, arithmetic and copies ran while one was open for 0% -> 1% of each run, Pallas kernels for 0% -> 0%
where the time goes in v1:
time: 398 us
  waiting for transfers between devices  287 us (72%)
  starting transfers between devices  38.7 us (10%)
  local copies, waits for them, and re-layouts  33.1 us (8%)
  matrix products  27.6 us (7%)
  other arithmetic  9.34 us (2%)
    all_to_all x1, waiting for transfers between devices, body(): lax.all_to_all(feature_send, 'dp', split_axis=1, concat_axis=1, tiled=True)  96 us
    all_to_all x1, waiting for transfers between devices, body(): lax.all_to_all(partial_out.astype(jnp.bfloat16), 'dp', split_axis=1, conc...  95.6 us
    all_to_all x1, waiting for transfers between devices, supply_all_records(): placed = jax.lax.all_to_all(val2, 'dp', 0, 0)  94.9 us
    unnamed x45, local copies, waits for them, and re-layouts  25.5 us
    all_to_all x1, starting transfers between devices, body(): lax.all_to_all(partial_out.astype(jnp.bfloat16), 'dp', split_axis=1, conc...  22.2 us
    dot_general x8, matrix products, add_group(): jnp.einsum('tsb,tsc->sbc', x_group, g_group, preferred_element_type=jnp.f...  15.6 us
    all_to_all x1, starting transfers between devices, supply_all_records(): placed = jax.lax.all_to_all(val2, 'dp', 0, 0)  11.6 us
  transfers between devices with their start and end apart: 3, of which 3 were waited for; matrix products, arithmetic and copies ran while one was open for 1% of the time, Pallas kernels for 0%

profile of v1, /device:TPU:4, one launch (start us, length us, event | category | flops | bytes accessed | tf_op | source)
XLA Modules:
  0.0 397.6 jit_solution(16973208922940132974)
XLA Ops:
  0.6 2.3 copy.115
  24.5 11.6 %all-to-all-start.1 = ((bf16[32,128,1,512]{3,1,2,0:T(8,128)(2,1)}), bf16[32,128,1,512]{3,1,2,0:T(8,128)(2,1)}, u32[]{:S(2)}, u32[]{:S(2)}) async-start(bf16[32,128,1,512]{3,1,2,0:T(8,128)(2,1)} %fusion.105), calls=%async_computation.1 | async-start | bytes 8388608 | tf_op jit(solution)/shard_map/all_to_all | solution.py:15
  36.1 1.8 copy.63
  37.9 94.9 %all-to-all-done.1 = bf16[32,128,1,512]{3,1,2,0:T(8,128)(2,1)} async-done(((bf16[32,128,1,512]{3,1,2,0:T(8,128)(2,1)}), bf16[32,128,1,512]{3,1,2,0:T(8,128)(2,1)}, u32[]{:S(2)}, u32[]{:S(2)}) %all-to-all-start.1) | async-done | bytes 4194336 | tf_op jit(solution)/shard_map/all_to_all | solution.py:15
  132.8 2.4 broadcast_in_dim.26
  135.2 4.9 %all-to-all-start = ((bf16[128,32,512]{2,0,1:T(8,128)(2,1)}), bf16[128,32,512]{2,0,1:T(8,128)(2,1)}, u32[]{:S(2)}, u32[]{:S(2)}) async-start(bf16[128,32,512]{2,0,1:T(8,128)(2,1)} %bitcast.214), calls=%async_computation | async-start | bytes 8388608 | tf_op jit(solution)/shard_map/all_to_all | solution.py:62
  140.8 96.0 %all-to-all-done = bf16[128,32,512]{2,0,1:T(8,128)(2,1)} async-done(((bf16[128,32,512]{2,0,1:T(8,128)(2,1)}), bf16[128,32,512]{2,0,1:T(8,128)(2,1)}, u32[]{:S(2)}, u32[]{:S(2)}) %all-to-all-start) | async-done | bytes 4194336 | tf_op jit(solution)/shard_map/all_to_all | solution.py:62
  236.8 21.4 %while.14 = (s32[]{:T(128)}, f32[512,512]{1,0:T(8,128)S(1)}, bf16[128,32,512]{2,0,1:T(8,128)(2,1)}, bf16[128,32,512]{2,0,1:T(8,128)(2,1)}, s32[]{:T(128)}, /*index=5*/s32[]{:T(128)}, s32[]{:T(128)}, s32[]{:T(128)}) while((s32[]{:T(128)}, f32[512,512]{1,0:T(8,128)S(1)}, bf16[128,32,512]{2,0,1:T(8,128)(2,1)}, ...), condition=%wide.region_2.0_spmd.clone, body=%wide.region_0.0_spmd.clone.sunk | while | flops 272891904 | bytes 9438349 | solution.py:77
  236.8 2.0 multiply_convert_fusion.2
  239.5 2.0 multiply_convert_fusion.2
  242.2 2.0 multiply_convert_fusion.2
  244.8 2.0 multiply_convert_fusion.2
  247.5 2.0 multiply_convert_fusion.2
  250.2 2.0 multiply_convert_fusion.2
  252.9 2.0 multiply_convert_fusion.2
  255.5 2.0 multiply_convert_fusion.2
  258.2 1.8 fusion.98
  261.6 2.2 conditional.1
  261.6 1.2 copy.104
  264.7 2.7 multiply_reduce_fusion.2
  268.1 6.9 %convert_bitcast_fusion = bf16[128,32,512]{0,2,1:T(8,128)(2,1)} fusion(bf16[128,32,512]{2,0,1:T(8,128)(2,1)} %all-to-all-done, f32[512,512]{1,0:T(8,128)S(1)} %get-tuple-element.156, f32[1,512,512]{2,1,0:T(8,128)} %param.14, f32[]{:T(128)S(6)} %div.14), kind=kOutput, calls=%fused_computation.69 | convolution fusion | flops 2150629376 | bytes 10485764 | tf_op jit(solution)/shard_map/tsb,bc->tsc/dot_general | solution.py:90
  275.0 22.2 %all-to-all-start.2 = ((bf16[128,32,512]{0,2,1:T(8,128)(2,1)}), bf16[128,32,512]{0,2,1:T(8,128)(2,1)}, u32[]{:S(2)}, u32[]{:S(2)}) async-start(bf16[128,32,512]{0,2,1:T(8,128)(2,1)} %convert_bitcast_fusion), calls=%async_computation.2 | async-start | bytes 8388608 | tf_op jit(solution)/shard_map/all_to_all | solution.py:93
  298.3 95.6 %all-to-all-done.2 = bf16[128,32,512]{0,2,1:T(8,128)(2,1)} async-done(((bf16[128,32,512]{0,2,1:T(8,128)(2,1)}), bf16[128,32,512]{0,2,1:T(8,128)(2,1)}, u32[]{:S(2)}, u32[]{:S(2)}) %all-to-all-start.2) | async-done | bytes 4194336 | tf_op jit(solution)/shard_map/all_to_all | solution.py:93
  393.9 2.9 reduce
  (67 shorter events, 32.2 us)
Async XLA Ops:
  0.6 2.3 copy-start.9
  24.5 108.3 %all-to-all-start.1 = ((bf16[32,128,1,512]{3,1,2,0:T(8,128)(2,1)}), bf16[32,128,1,512]{3,1,2,0:T(8,128)(2,1)}, u32[]{:S(2)}, u32[]{:S(2)}) async-start(bf16[32,128,1,512]{3,1,2,0:T(8,128)(2,1)} %fusion.105), calls=%async_computation.1 | async-start | bytes 8388608 | tf_op jit(solution)/shard_map/all_to_all | solution.py:15
  135.2 101.6 %all-to-all-start = ((bf16[128,32,512]{2,0,1:T(8,128)(2,1)}), bf16[128,32,512]{2,0,1:T(8,128)(2,1)}, u32[]{:S(2)}, u32[]{:S(2)}) async-start(bf16[128,32,512]{2,0,1:T(8,128)(2,1)} %bitcast.214), calls=%async_computation | async-start | bytes 8388608 | tf_op jit(solution)/shard_map/all_to_all | solution.py:62
  258.2 1.9 copy-start.8
  258.2 2.4 copy-start.2
  260.1 1.0 copy-start.3
  260.6 1.0 copy-start.4
  263.8 1.0 copy-start.7
  275.0 118.9 %all-to-all-start.2 = ((bf16[128,32,512]{0,2,1:T(8,128)(2,1)}), bf16[128,32,512]{0,2,1:T(8,128)(2,1)}, u32[]{:S(2)}, u32[]{:S(2)}) async-start(bf16[128,32,512]{0,2,1:T(8,128)(2,1)} %convert_bitcast_fusion), calls=%async_computation.2 | async-start | bytes 8388608 | tf_op jit(solution)/shard_map/all_to_all | solution.py:93
